TPU v7x, 32 devices: a whole 2x2x4 slice. The times are simulated.
32 devices in a mesh: batch: 8 (over z, y), mp: 4 (over x, core).
Axes of the slice: x: 2, y: 2, z: 4, core: 2. Of those that a mesh axis runs over, the one named last changes fastest.
Arguments:
- gate_act: bfloat16 [6144, 14336], P('batch', 'mp'), may hold values from -6 to 6
- up_act: bfloat16 [6144, 14336], P('batch', 'mp'), may hold values from -6 to 6
- upstream: bfloat16 [6144, 8192], P('batch', 'mp'), may hold values from -6 to 6
- kept_index: int32 [8, 8], P('batch'), may hold values from 0 to 31, as said below
- kept_count: int32 [8], P('batch'), may hold values from 1 to 8, as said below
Outputs:
- grad_down: bfloat16 [8192, 14336], P('batch', 'mp')
Inputs may be any that keep to these rules, and one draw needn't show every extreme that they name: `kept_index`: each group's row names different candidates; only the first kept_count entries of a row are kept. `kept_count`: the counts sum to 8 * 4 over the groups, and some group keeps exactly 8.
All inputs are finite; a program needn't handle non-finite values.
Results may differ from a plain program's by a relative error of at most 0.0049.
Values may be sent and summed in bfloat16 or wider, within the bound.
A program may use at most 128 MiB of HBM per device.

v0:
```python
import math
import jax
import jax.numpy as jnp
from jax import lax
from jax.sharding import PartitionSpec as P

SEQ = 24
CAND = 32


def on_device(gate_act, up_act, upstream, kept_index, kept_count):
    groups = lax.axis_size("batch")
    share = groups // 2
    keep_most = kept_index.shape[1]
    hidden_width = gate_act.shape[1]
    model_part = upstream.shape[1]
    gate_all = gate_act.reshape(CAND, SEQ, hidden_width)
    up_all = up_act.reshape(CAND, SEQ, hidden_width)
    grad_all = upstream.reshape(CAND, SEQ, model_part)
    picked = kept_index[0]
    counts = lax.all_gather(kept_count, "batch", axis=0, tiled=True)
    starts = jnp.cumsum(counts) - counts
    myself = lax.axis_index("batch")
    targets = jnp.arange(groups, dtype=jnp.int32)
    my_slot = jnp.mod(targets - starts[myself], groups)
    present = my_slot < counts[myself]
    seq_ids = picked[jnp.minimum(my_slot, keep_most - 1)]
    hidden = (
        jax.nn.silu(gate_all[seq_ids].astype(jnp.float32)) * up_all[seq_ids].astype(jnp.float32)
    ).astype(jnp.bfloat16)
    hidden_out = jnp.where(present[:, None, None], hidden, jnp.zeros_like(hidden))
    grad_out = grad_all[seq_ids]
    hidden_in, grad_in = (
        lax.all_to_all(hidden_out, "batch", split_axis=0, concat_axis=0, tiled=True),
        lax.all_to_all(grad_out, "batch", split_axis=0, concat_axis=0, tiled=True),
    )
    arrived = jnp.mod(myself - starts, groups) < counts
    chosen = jnp.argsort(1 - arrived.astype(jnp.int32), stable=True)[:share]
    hidden_rows = hidden_in[chosen].reshape(share * SEQ, hidden_width)
    grad_rows = grad_in[chosen].reshape(share * SEQ, model_part)
    full_width = lax.all_gather(grad_rows, "mp", axis=1, tiled=True)
    columns = lax.all_to_all(full_width, "batch", split_axis=1, concat_axis=0, tiled=True)
    summed = lax.dot_general(
        columns,
        lax.all_gather(hidden_rows, "batch", axis=0, tiled=True),
        (((0,), (0,)), ((), ())),
        preferred_element_type=jnp.float32,
    )
    factor = 1.0 / math.sqrt(groups * share * SEQ)
    return (summed * factor).astype(jnp.bfloat16)


def solution(mesh):
    placed = (P("batch", "mp"), P("batch", "mp"), P("batch", "mp"), P("batch", None), P("batch"))
    return jax.shard_map(
        on_device, mesh=mesh, in_specs=placed, out_specs=P("batch", "mp"), check_vma=False
    )
```

profile of v0, /device:TPU:0, one launch (start us, length us, event | category | flops | bytes accessed | tf_op | source)
XLA Modules:
  0.0 218.1 jit_solution(4112580387159058532)
XLA Ops:
  6.5 0.0 copy-start
  7.3 1.4 dynamic-slice
  8.7 0.8 dynamic-update-slice
  9.5 13.1 %all-reduce = s32[8]{0:T(128)S(1)} all-reduce(s32[8]{0:T(128)S(1)} %dynamic-update-slice), channel_id=1, replica_groups=mesh['batch'=8,'mp'=4] {'batch'}, use_global_device_ids=true, to_apply=%add | all-reduce | flops 8 | bytes 64
  22.6 0.2 reduce-window.9
  22.8 0.6 dynamic_slice.6
  23.4 0.6 fusion.11
  23.9 1.3 gather_fusion
  25.3 0.0 copy-done
  25.3 1.5 gather_fusion.1
  26.8 4.2 %all-to-all-start = ((bf16[8,24,2048]{2,1,0:T(8,128)(2,1)}), bf16[8,24,2048]{2,1,0:T(8,128)(2,1)}, u32[]{:S(2)}, u32[]{:S(2)}) async-start(bf16[8,24,2048]{2,1,0:T(8,128)(2,1)} %gather_fusion.1), calls=%async_computation | async-start | bytes 1572864 | tf_op jit(solution)/shard_map/all_to_all | solution.py:35
  31.0 0.6 dynamic_slice.7
  31.6 4.3 %gather_fusion.4 = bf16[8,24,3584]{2,1,0:T(8,128)(2,1)} fusion(bf16[32,24,3584]{2,1,0:T(8,128)(2,1)} %bitcast.35, s32[1024]{0:T(1024)S(1)} %pad_clamp_fusion.1), kind=kCustom, calls=%fused_computation.4 | custom fusion | bytes 2752544 | tf_op jit(solution)/shard_map/gather | solution.py:29
  35.9 4.3 %gather_fusion.3 = bf16[8,24,3584]{2,1,0:T(8,128)(2,1)} fusion(bf16[32,24,3584]{2,1,0:T(8,128)(2,1)} %bitcast.36, s32[1024]{0:T(1024)S(1)} %pad_clamp_fusion.1), kind=kCustom, calls=%fused_computation.3 | custom fusion | bytes 2752544 | tf_op jit(solution)/shard_map/gather | solution.py:29
  40.2 0.9 sort.17
  41.1 1.2 fusion.7
  42.3 3.7 %fusion.5 = bf16[8,24,3584]{2,1,0:T(8,128)(2,1)} fusion(bf16[8,24,3584]{2,1,0:T(8,128)(2,1)} %gather_fusion.4, bf16[8,24,3584]{2,1,0:T(8,128)(2,1)} %gather_fusion.3, pred[8]{0:T(512)(128)(4,1)S(1)} %fusion.7), kind=kLoop, calls=%fused_computation.15 | loop fusion | flops 6193152 | bytes 4128776 | tf_op jit(solution)/shard_map/jit(_where)/select_n | solution.py:31
  46.1 2.6 %all-to-all-done = bf16[8,24,2048]{2,1,0:T(8,128)(2,1)} async-done(((bf16[8,24,2048]{2,1,0:T(8,128)(2,1)}), bf16[8,24,2048]{2,1,0:T(8,128)(2,1)}, u32[]{:S(2)}, u32[]{:S(2)}) %all-to-all-start) | async-done | bytes 786464 | tf_op jit(solution)/shard_map/all_to_all | solution.py:35
  48.6 4.3 %all-to-all-start.2 = ((bf16[8,24,3584]{2,1,0:T(8,128)(2,1)}), bf16[8,24,3584]{2,1,0:T(8,128)(2,1)}, u32[]{:S(2)}, u32[]{:S(2)}) async-start(bf16[8,24,3584]{2,1,0:T(8,128)(2,1)} %fusion.5), calls=%async_computation.2 | async-start | bytes 2752512 | tf_op jit(solution)/shard_map/all_to_all | solution.py:34
  52.9 0.0 all-gather.3.cloned.1.call-start
  53.0 2.5 %gather_fusion.2 = bf16[4,24,2048]{2,1,0:T(8,128)(2,1)} fusion(bf16[8,24,2048]{2,1,0:T(8,128)(2,1)} %all-to-all-done, s32[1024]{0:T(1024)S(1)} %pad_clamp_fusion), kind=kCustom, calls=%fused_computation.2 | custom fusion | bytes 786448 | tf_op jit(solution)/shard_map/gather | solution.py:40
  55.4 0.0 all-gather.3.cloned.1.call-update
  55.5 0.0 all-gather.5.cloned.1.call-start
  55.5 28.7 %all-to-all-done.2 = bf16[8,24,3584]{2,1,0:T(8,128)(2,1)} async-done(((bf16[8,24,3584]{2,1,0:T(8,128)(2,1)}), bf16[8,24,3584]{2,1,0:T(8,128)(2,1)}, u32[]{:S(2)}, u32[]{:S(2)}) %all-to-all-start.2) | async-done | bytes 1376288 | tf_op jit(solution)/shard_map/all_to_all | solution.py:34
  84.2 2.8 %gather_fusion.5 = bf16[4,24,3584]{2,1,0:T(8,128)(2,1)} fusion(bf16[8,24,3584]{2,1,0:T(8,128)(2,1)} %all-to-all-done.2, s32[1024]{0:T(1024)S(1)} %pad_clamp_fusion), kind=kCustom, calls=%fused_computation.5 | custom fusion | bytes 1376272 | tf_op jit(solution)/shard_map/gather | solution.py:39
  87.0 0.0 all-gather.5.cloned.1.call-update
  87.0 0.0 all-gather.3.cloned.1.call-done
  87.0 1.5 copy.10
  88.6 62.6 %all_to_all.29 = bf16[96,8,1024]{2,0,1:T(8,128)(2,1)} all-to-all(bf16[96,8,1024]{2,0,1:T(8,128)(2,1)S(1)} %bitcast.30), channel_id=1, replica_groups=mesh['batch'=8,'mp'=4] {'batch'}, dimensions={1} | all-to-all | bytes 3145728 | tf_op jit(solution)/shard_map/all_to_all | solution.py:42
  151.2 49.8 %all-gather.5.cloned.1.call-done = bf16[768,3584]{1,0:T(8,128)(2,1)} async-done(((bf16[96,3584]{1,0:T(8,128)(2,1)}), bf16[768,3584]{1,0:T(8,128)(2,1)}) %all-gather.5.cloned.1.call-update) | async-done | bytes 5505040 | tf_op jit(solution)/shard_map/all_gather | solution.py:45
  201.0 10.2 %multiply_convert_fusion = bf16[1024,3584]{1,0:T(8,128)(2,1)} fusion(bf16[768,1024]{1,0:T(8,128)(2,1)} %bitcast.33, bf16[768,3584]{1,0:T(8,128)(2,1)} %all-gather.5.cloned.1.call-done), kind=kOutput, calls=%fused_computation.6 | convolution fusion | flops 5644484608 | bytes 14417920 | tf_op jit(solution)/shard_map/dot_general | solution.py:43
  (8 shorter events, 0.1 us)
Async XLA Ops:
  6.5 18.7 %copy-start = (bf16[768,2048]{1,0:T(8,128)(2,1)S(1)}, bf16[768,2048]{1,0:T(8,128)(2,1)}, u32[]{:S(2)}) copy-start(bf16[768,2048]{1,0:T(8,128)(2,1)} %param.7) | copy-start | bytes 9437188
  26.8 21.9 %all-to-all-start = ((bf16[8,24,2048]{2,1,0:T(8,128)(2,1)}), bf16[8,24,2048]{2,1,0:T(8,128)(2,1)}, u32[]{:S(2)}, u32[]{:S(2)}) async-start(bf16[8,24,2048]{2,1,0:T(8,128)(2,1)} %gather_fusion.1), calls=%async_computation | async-start | bytes 1572864 | tf_op jit(solution)/shard_map/all_to_all | solution.py:35
  48.6 35.6 %all-to-all-start.2 = ((bf16[8,24,3584]{2,1,0:T(8,128)(2,1)}), bf16[8,24,3584]{2,1,0:T(8,128)(2,1)}, u32[]{:S(2)}, u32[]{:S(2)}) async-start(bf16[8,24,3584]{2,1,0:T(8,128)(2,1)} %fusion.5), calls=%async_computation.2 | async-start | bytes 2752512 | tf_op jit(solution)/shard_map/all_to_all | solution.py:34
  52.9 34.1 %all-gather.3.cloned.1.call-start = ((), (), s32[]{:S(2)}) async-start(), calls=%async_computation.3 | async-start | bytes 1966080 | tf_op jit(solution)/shard_map/all_gather | solution.py:41
  55.5 145.6 %all-gather.5.cloned.1.call-start = ((), (), s32[]{:S(2)}) async-start(), calls=%async_computation.4 | async-start | bytes 6193152 | tf_op jit(solution)/shard_map/all_gather | solution.py:45
Sparse Core Ops, SparseCore 0:
  55.6 20.8 all-gather.2
  87.1 113.8 all-gather.4
where the time goes:
time: 219 us; the launch traced here: 218 us
  waiting for transfers between devices  81.2 us (37%)
  blocking collectives  75.7 us (35%)
  local copies, waits for them, and re-layouts  21.5 us (10%)
  between operations  14.3 us (7%)
  matrix products  10.2 us (5%)
  starting transfers between devices  8.57 us (4%)
  other arithmetic  6.7 us (3%)
    all_to_all x1, blocking collectives, on_device(): lax.all_to_all(full_width, 'batch', split_axis=1, concat_axis=0, tiled=True)  62.6 us
    all_gather x1, waiting for transfers between devices, on_device(): lax.all_gather(hidden_rows, 'batch', axis=0, tiled=True)  49.8 us
    all_to_all x1, waiting for transfers between devices, on_device(): lax.all_to_all(hidden_out, 'batch', split_axis=0, concat_axis=0, tiled=True)  28.7 us
    unnamed x1, blocking collectives  13.1 us
    dot_general x1, matrix products, on_device(): lax.dot_general(columns, lax.all_gather(hidden_rows, 'batch', axis=0, til...  10.2 us
  transfers between devices with their start and end apart: 4, of which 3 were waited for; matrix products, arithmetic and copies ran while one was open for 10% of the time, Pallas kernels for 0%

commit v1 on v0

--- a/solution.py
+++ b/solution.py
@@ -40,9 +40,18 @@
     grad_rows = grad_in[chosen].reshape(share * SEQ, model_part)
     full_width = lax.all_gather(grad_rows, "mp", axis=1, tiled=True)
     columns = lax.all_to_all(full_width, "batch", split_axis=1, concat_axis=0, tiled=True)
+
+    def reach_the_stages_all(block_in, across):
+        trail = []
+        for _ in range(lax.axis_size(across)):
+            trail.append(block_in)
+        big = jnp.stack(trail, 0)
+        opened = lax.all_to_all(big, across, 0, 0)
+        return jnp.concatenate(opened, 0)
+
     summed = lax.dot_general(
         columns,
-        lax.all_gather(hidden_rows, "batch", axis=0, tiled=True),
+        reach_the_stages_all(hidden_rows, across="batch"),
         (((0,), (0,)), ((), ())),
         preferred_element_type=jnp.float32,
     )

time: 219 us -> 268 us (1.22)
  blocking collectives: 75.7 us -> 138 us
  waiting for transfers between devices: 81.2 us -> 62.1 us
  starting transfers between devices: 8.57 us -> 12.8 us
  local copies, waits for them, and re-layouts: 21.5 us -> 24.3 us
    all_to_all x1, blocking collectives: 62.6 us -> 125 us  [reach_the_stages_all(): opened = lax.all_to_all(big, across, 0, 0)]
    all_gather x1 -> x0, waiting for transfers between devices: 49.8 us -> none  [on_device(): lax.all_gather(hidden_rows, 'batch', axis=0, tiled=True)]
    all_to_all x0 -> x1, waiting for transfers between devices: none -> 33.6 us  [on_device(): lax.all_to_all(full_width, 'batch', split_axis=1, concat_axis=0, tiled=True)]
    all_to_all x1, waiting for transfers between devices: 28.7 us -> 5 us  [on_device(): lax.all_to_all(hidden_out, 'batch', split_axis=0, concat_axis=0, tiled=True)]
    all_gather x1, waiting for transfers between devices: 0.02 us -> 21.1 us  [on_device(): full_width = lax.all_gather(grad_rows, 'mp', axis=1, tiled=True)]
    all_to_all x0 -> x1, starting transfers between devices: none -> 4.29 us  [on_device(): lax.all_to_all(full_width, 'batch', split_axis=1, concat_axis=0, tiled=True)]
  transfers between devices with their start and end apart: 4 -> 4, of which waited for: 3 -> 4; matrix products, arithmetic and copies ran while one was open for 10% -> 9% of each run, Pallas kernels for 0% -> 0%
where the time goes in v1:
time: 268 us
  blocking collectives  138 us (51%)
  waiting for transfers between devices  62.1 us (23%)
  local copies, waits for them, and re-layouts  24.3 us (9%)
  between operations  14.3 us (5%)
  starting transfers between devices  12.8 us (5%)
  matrix products  9.48 us (4%)
  other arithmetic  6.84 us (3%)
    all_to_all x1, blocking collectives, reach_the_stages_all(): opened = lax.all_to_all(big, across, 0, 0)  125 us
    all_to_all x1, waiting for transfers between devices, on_device(): lax.all_to_all(full_width, 'batch', split_axis=1, concat_axis=0, tiled=True)  33.6 us
    all_gather x1, waiting for transfers between devices, on_device(): full_width = lax.all_gather(grad_rows, 'mp', axis=1, tiled=True)  21.1 us
    unnamed x1, blocking collectives  13.1 us
    dot_general x1, matrix products, on_device(): lax.dot_general(columns, reach_the_stages_all(hidden_rows, across='batch'...  9.48 us
  transfers between devices with their start and end apart: 4, of which 4 were waited for; matrix products, arithmetic and copies ran while one was open for 9% of the time, Pallas kernels for 0%

profile of v1, /device:TPU:0, one launch (start us, length us, event | category | flops | bytes accessed | tf_op | source)
XLA Modules:
  0.0 267.7 jit_solution(13873027729200605351)
XLA Ops:
  6.5 0.0 copy-start
  7.3 1.4 dynamic-slice
  8.7 0.8 dynamic-update-slice
  9.5 13.1 %all-reduce = s32[8]{0:T(128)S(1)} all-reduce(s32[8]{0:T(128)S(1)} %dynamic-update-slice), channel_id=1, replica_groups=mesh['batch'=8,'mp'=4] {'batch'}, use_global_device_ids=true, to_apply=%add | all-reduce | flops 8 | bytes 64
  22.6 0.2 reduce-window.9
  22.8 0.6 dynamic_slice.6
  23.4 0.6 fusion.13
  24.0 1.3 gather_fusion
  25.3 0.0 copy-done
  25.4 1.5 gather_fusion.1
  26.9 4.2 %all-to-all-start = ((bf16[8,24,2048]{2,1,0:T(8,128)(2,1)}), bf16[8,24,2048]{2,1,0:T(8,128)(2,1)}, u32[]{:S(2)}, u32[]{:S(2)}) async-start(bf16[8,24,2048]{2,1,0:T(8,128)(2,1)} %gather_fusion.1), calls=%async_computation | async-start | bytes 1572864 | tf_op jit(solution)/shard_map/all_to_all | solution.py:35
  31.1 0.7 dynamic_slice.7
  31.7 4.3 %gather_fusion.4 = bf16[8,24,3584]{2,1,0:T(8,128)(2,1)} fusion(bf16[32,24,3584]{2,1,0:T(8,128)(2,1)} %bitcast.37, s32[1024]{0:T(1024)S(1)} %pad_clamp_fusion.1), kind=kCustom, calls=%fused_computation.4 | custom fusion | bytes 2752544 | tf_op jit(solution)/shard_map/gather | solution.py:29
  36.0 4.3 %gather_fusion.3 = bf16[8,24,3584]{2,1,0:T(8,128)(2,1)} fusion(bf16[32,24,3584]{2,1,0:T(8,128)(2,1)} %bitcast.38, s32[1024]{0:T(1024)S(1)} %pad_clamp_fusion.1), kind=kCustom, calls=%fused_computation.3 | custom fusion | bytes 2752544 | tf_op jit(solution)/shard_map/gather | solution.py:29
  40.3 1.0 sort.17
  41.3 1.3 fusion.9
  42.5 3.8 %fusion.7 = bf16[8,24,3584]{2,1,0:T(8,128)(2,1)} fusion(bf16[8,24,3584]{2,1,0:T(8,128)(2,1)} %gather_fusion.4, bf16[8,24,3584]{2,1,0:T(8,128)(2,1)} %gather_fusion.3, pred[8]{0:T(512)(128)(4,1)S(1)} %fusion.9), kind=kLoop, calls=%fused_computation.17 | loop fusion | flops 6193152 | bytes 4128776 | tf_op jit(solution)/shard_map/jit(_where)/select_n | solution.py:31
  46.3 2.4 all-to-all-done
  48.7 4.3 %all-to-all-start.2 = ((bf16[8,24,3584]{2,1,0:T(8,128)(2,1)}), bf16[8,24,3584]{2,1,0:T(8,128)(2,1)}, u32[]{:S(2)}, u32[]{:S(2)}) async-start(bf16[8,24,3584]{2,1,0:T(8,128)(2,1)} %fusion.7), calls=%async_computation.2 | async-start | bytes 2752512 | tf_op jit(solution)/shard_map/all_to_all | solution.py:34
  53.0 0.0 all-gather.2.cloned.1.call-start
  53.0 2.5 gather_fusion.2
  55.5 0.0 all-gather.2.cloned.1.call-update
  55.5 21.1 %all-gather.2.cloned.1.call-done = bf16[96,8192]{1,0:T(8,128)(2,1)} async-done(((bf16[96,2048]{1,0:T(8,128)(2,1)}), bf16[96,8192]{1,0:T(8,128)(2,1)}) %all-gather.2.cloned.1.call-update) | async-done | bytes 1572880 | tf_op jit(solution)/shard_map/all_gather | solution.py:41
  76.6 2.7 %copy.9 = bf16[12,8,8,1024]{3,2,0,1:T(8,128)(2,1)} copy(bf16[12,8,8,1024]{3,2,1,0:T(8,128)(2,1)} %bitcast.35) | data formatting | bytes 3145728 | tf_op jit(solution)/shard_map/all_to_all | solution.py:42
  79.3 5.0 %all-to-all-done.2 = bf16[8,24,3584]{2,1,0:T(8,128)(2,1)} async-done(((bf16[8,24,3584]{2,1,0:T(8,128)(2,1)}), bf16[8,24,3584]{2,1,0:T(8,128)(2,1)}, u32[]{:S(2)}, u32[]{:S(2)}) %all-to-all-start.2) | async-done | bytes 1376288 | tf_op jit(solution)/shard_map/all_to_all | solution.py:34
  84.3 4.3 %all-to-all-start.1 = ((bf16[96,8,1024]{2,0,1:T(8,128)(2,1)}), bf16[96,8,1024]{2,0,1:T(8,128)(2,1)}, u32[]{:S(2)}, u32[]{:S(2)}) async-start(bf16[96,8,1024]{2,0,1:T(8,128)(2,1)} %bitcast.33), calls=%async_computation.1 | async-start | bytes 3145728 | tf_op jit(solution)/shard_map/all_to_all | solution.py:42
  88.6 2.8 %gather_fusion.5 = bf16[4,24,3584]{2,1,0:T(8,128)(2,1)} fusion(bf16[8,24,3584]{2,1,0:T(8,128)(2,1)} %all-to-all-done.2, s32[1024]{0:T(1024)S(1)} %pad_clamp_fusion), kind=kCustom, calls=%fused_computation.5 | custom fusion | bytes 1376272 | tf_op jit(solution)/shard_map/gather | solution.py:39
  91.4 33.6 %all-to-all-done.1 = bf16[96,8,1024]{2,0,1:T(8,128)(2,1)} async-done(((bf16[96,8,1024]{2,0,1:T(8,128)(2,1)}), bf16[96,8,1024]{2,0,1:T(8,128)(2,1)}, u32[]{:S(2)}, u32[]{:S(2)}) %all-to-all-start.1) | async-done | bytes 1572896 | tf_op jit(solution)/shard_map/all_to_all | solution.py:42
  125.0 1.6 stack.3
  126.6 124.8 %all_to_all.31 = bf16[8,96,3584]{2,1,0:T(8,128)(2,1)S(1)} all-to-all(bf16[8,96,3584]{2,1,0:T(8,128)(2,1)S(1)} %stack.3), channel_id=1, replica_groups=mesh['batch'=8,'mp'=4] {'batch'}, dimensions={0} | all-to-all | bytes 11010048 | tf_op jit(solution)/shard_map/all_to_all | solution.py:49
  251.4 9.5 %fusion = bf16[1024,3584]{1,0:T(8,128)(2,1)} fusion(bf16[8,96,3584]{2,1,0:T(8,128)(2,1)S(1)} %all_to_all.31, bf16[96,8,1024]{2,0,1:T(8,128)(2,1)} %all-to-all-done.1), kind=kOutput, calls=%fused_computation.7 | convolution fusion | flops 5644484608 | bytes 14417920 | tf_op jit(solution)/shard_map/dot_general | solution.py:52
  (8 shorter events, 0.1 us)
Async XLA Ops:
  6.5 18.8 %copy-start = (bf16[768,2048]{1,0:T(8,128)(2,1)S(1)}, bf16[768,2048]{1,0:T(8,128)(2,1)}, u32[]{:S(2)}) copy-start(bf16[768,2048]{1,0:T(8,128)(2,1)} %param.7) | copy-start | bytes 9437188
  26.9 21.8 %all-to-all-start = ((bf16[8,24,2048]{2,1,0:T(8,128)(2,1)}), bf16[8,24,2048]{2,1,0:T(8,128)(2,1)}, u32[]{:S(2)}, u32[]{:S(2)}) async-start(bf16[8,24,2048]{2,1,0:T(8,128)(2,1)} %gather_fusion.1), calls=%async_computation | async-start | bytes 1572864 | tf_op jit(solution)/shard_map/all_to_all | solution.py:35
  48.7 35.6 %all-to-all-start.2 = ((bf16[8,24,3584]{2,1,0:T(8,128)(2,1)}), bf16[8,24,3584]{2,1,0:T(8,128)(2,1)}, u32[]{:S(2)}, u32[]{:S(2)}) async-start(bf16[8,24,3584]{2,1,0:T(8,128)(2,1)} %fusion.7), calls=%async_computation.2 | async-start | bytes 2752512 | tf_op jit(solution)/shard_map/all_to_all | solution.py:34
  53.0 23.6 %all-gather.2.cloned.1.call-start = ((), (), s32[]{:S(2)}) async-start(), calls=%async_computation.4 | async-start | bytes 1966080 | tf_op jit(solution)/shard_map/all_gather | solution.py:41
  84.3 40.7 %all-to-all-start.1 = ((bf16[96,8,1024]{2,0,1:T(8,128)(2,1)}), bf16[96,8,1024]{2,0,1:T(8,128)(2,1)}, u32[]{:S(2)}, u32[]{:S(2)}) async-start(bf16[96,8,1024]{2,0,1:T(8,128)(2,1)} %bitcast.33), calls=%async_computation.1 | async-start | bytes 3145728 | tf_op jit(solution)/shard_map/all_to_all | solution.py:42
Sparse Core Ops, SparseCore 0:
  55.6 20.8 all-gather.1
